TPU v7x, 32 devices: a whole 2x2x4 slice. The times are simulated.
32 devices in a mesh: grp: 2 (over x), seq: 16 (over z, y, core).
Axes of the slice: x: 2, y: 2, z: 4, core: 2. Of those that a mesh axis runs over, the one named last changes fastest.
Arguments:
- image_qkv: bfloat16 [3, 8, 16, 896, 128], P(None, 'grp', None, 'seq'), parts along dimension 1, may hold values from -16 to 16
- text_kv: bfloat16 [2, 2, 8, 16, 512, 128], P(None, None, 'grp', None, 'seq'), parts along dimension 2, may hold values from -6 to 6
- prompt_ids: int32 [2, 8, 512], P(None, 'grp'), parts along dimension 1, may hold values from 0 to 32127, as said below
- timesteps: int32 [8], P('grp'), parts along dimension 0, may hold values from 0 to 999
- image_states: bfloat16 [8, 896, 1536], P('grp', 'seq'), parts along dimension 0, may hold values from -6 to 6
- frozen_out: bfloat16 [2048, 1536], P('seq'), may hold values from -0.125 to 0.125
- trainee_out: bfloat16 [4096, 1536], P(('grp', 'seq')), parts along dimension 0, may hold values from -0.125 to 0.125
- time_mod: bfloat16 [256, 3072], replicated, may hold values from -0.375 to 0.375
- final_head: bfloat16 [1536, 64], replicated, may hold values from -0.15625 to 0.15625
Outputs:
- weight_grad: float32 [4096, 1536], P(('grp', 'seq')), parts along dimension 0
There are 2 independent parts, one for each index of `grp`. A program takes and returns all parts, laid end to end along the dimension named above; an argument that names none is the same for every part. Nothing has to cross between parts.
Inputs may be any that keep to these rules, and one draw needn't show every extreme that they name: `prompt_ids`: zero marks padding; in each row of 512 ids the padding is a suffix and position 0 is never padding.
All inputs are finite; a program needn't handle non-finite values.
Results may differ from a plain program's by a relative error of at most 0.011.
Values may be sent and summed in bfloat16 or wider, within the bound.
No kernel may reach another device: no remote copies, remote signals or barrier semaphores. Data moves between devices by JAX's collectives and lax.ppermute only.
A program may use at most 128 MiB of HBM per device.

v0:
```python
import math
import jax
import jax.numpy as jnp
from jax import lax
from jax.sharding import PartitionSpec as P

SAMPLES = 4
HEADS = 16
HEAD_DIM = 128
WIDTH = 1536
TIME_DIM = 256


def image_block(queries, image_keys, image_values):
    factor = HEAD_DIM ** (-0.5)
    image_scores = jnp.dot(queries, image_keys.T, preferred_element_type=jnp.float32) * factor
    image_max = jnp.max(image_scores, axis=1, keepdims=True)
    image_exp = jnp.exp(image_scores - image_max)
    image_total = jnp.sum(image_exp, axis=1, keepdims=True)
    image_part = jnp.dot(
        image_exp.astype(jnp.bfloat16), image_values, preferred_element_type=jnp.float32
    )
    return (image_max, image_total, image_part)


def text_finish(queries, image_stats, text_keys, text_values, allowed_text):
    factor = HEAD_DIM ** (-0.5)
    image_max, image_total, image_part = image_stats
    text_scores = jnp.dot(queries, text_keys.T, preferred_element_type=jnp.float32) * factor
    text_scores = jnp.where(allowed_text[None, :], text_scores, -jnp.inf)
    pass_max = jnp.maximum(image_max, jnp.max(text_scores, axis=1, keepdims=True))
    ratio = jnp.exp(image_max - pass_max)
    text_exp = jnp.exp(text_scores - pass_max)
    text_part = jnp.dot(
        text_exp.astype(jnp.bfloat16), text_values, preferred_element_type=jnp.float32
    )
    numer = ratio * image_part + text_part
    denom = ratio * image_total + jnp.sum(text_exp, axis=1, keepdims=True)
    return (numer / denom).astype(jnp.bfloat16)


def head_out(branch, states, gate, scale, final_head):
    mixed = states.astype(jnp.float32) + gate[:, None, :] * branch
    normed = (
        mixed
        * lax.rsqrt(jnp.mean(mixed * mixed, axis=-1, keepdims=True) + 1e-06)
        * (1.0 + scale[:, None, :])
    )
    normed = normed.astype(jnp.bfloat16)
    return jnp.einsum("bic,cd->bid", normed, final_head, preferred_element_type=jnp.float32)


def shards(
    image_qkv,
    text_kv,
    prompt_ids,
    timesteps,
    image_states,
    frozen_out,
    trainee_out,
    time_mod,
    final_head,
):
    group_size = lax.axis_size("seq")
    position = lax.axis_index("seq")
    image_dev = image_qkv.shape[3]
    text_dev = text_kv.shape[4]
    item_count = SAMPLES * HEADS
    owned_count = item_count // group_size
    token_rows = SAMPLES * image_dev
    image_all = image_dev * group_size
    block_rows = image_dev * min(group_size, 8)
    block_count = image_all // block_rows
    image_local = image_qkv.transpose(0, 2, 1, 3, 4).reshape(3, item_count, image_dev, HEAD_DIM)
    text_local = text_kv.transpose(0, 1, 3, 2, 4, 5).reshape(4, item_count, text_dev, HEAD_DIM)
    image_heads, text_heads = (
        lax.all_to_all(image_local, "seq", split_axis=1, concat_axis=2, tiled=True),
        lax.all_to_all(text_local, "seq", split_axis=1, concat_axis=2, tiled=True),
    )
    owned_items = position * owned_count + jnp.arange(owned_count, dtype=jnp.int32)
    sample_of = owned_items % SAMPLES
    selector = (sample_of[:, None] == jnp.arange(SAMPLES, dtype=jnp.int32)[None, :]).astype(
        jnp.float32
    )
    live_all = (prompt_ids != 0).astype(jnp.float32)
    live_owned = jnp.einsum("jb,pbt->pjt", selector, live_all) > 0.5

    def query_blocks(item_index):
        return image_heads[0, item_index].reshape(block_count, block_rows, HEAD_DIM)

    def joint_item(item_index):
        image_keys = image_heads[1, item_index]
        image_values = image_heads[2, item_index]

        def per_block(queries):
            stats = image_block(queries, image_keys, image_values)
            concept = text_finish(
                queries,
                stats,
                text_heads[0, item_index],
                text_heads[1, item_index],
                live_owned[0, item_index],
            )
            null = text_finish(
                queries,
                stats,
                text_heads[2, item_index],
                text_heads[3, item_index],
                live_owned[1, item_index],
            )
            return jnp.stack([concept, null])

        blocks = lax.map(per_block, query_blocks(item_index))
        return blocks.transpose(1, 0, 2, 3).reshape(2, image_all, HEAD_DIM)

    both_passes = lax.map(joint_item, jnp.arange(owned_count, dtype=jnp.int32)).transpose(
        1, 0, 2, 3
    )
    returned = lax.all_to_all(both_passes, "seq", split_axis=2, concat_axis=1, tiled=True)
    attention = returned.reshape(2, HEADS, SAMPLES, image_dev, HEAD_DIM).transpose(0, 2, 3, 1, 4)
    attention = attention.reshape(2, token_rows, HEADS * HEAD_DIM)
    half_dim = TIME_DIM // 2
    freqs = jnp.exp(-math.log(10000.0) * jnp.arange(half_dim, dtype=jnp.float32) / half_dim)
    angles = timesteps.astype(jnp.float32)[:, None] * freqs[None, :]
    embedding = jnp.concatenate([jnp.cos(angles), jnp.sin(angles)], 1)
    modulation = jnp.dot(embedding, time_mod.astype(jnp.float32), precision=lax.Precision.HIGHEST)
    gate = modulation[:, :WIDTH]
    scale = modulation[:, WIDTH:]
    piece_frozen = lax.all_gather(frozen_out, "seq", axis=0, tiled=True)
    piece_trainee = lax.all_gather(trainee_out, "seq", axis=0, tiled=True)
    columns_c = attention[0]
    columns_n = attention[1]
    branch_c = jnp.dot(columns_c, piece_frozen, preferred_element_type=jnp.float32)
    branch_n = jnp.dot(columns_n, piece_frozen, preferred_element_type=jnp.float32)
    branch_s = jnp.dot(columns_c, piece_trainee, preferred_element_type=jnp.float32)
    branch_c = branch_c.reshape(SAMPLES, image_dev, WIDTH)
    branch_n = branch_n.reshape(SAMPLES, image_dev, WIDTH)
    branch_s = branch_s.reshape(SAMPLES, image_dev, WIDTH)
    velocity_c = head_out(branch_c, image_states, gate, scale, final_head)
    velocity_n = head_out(branch_n, image_states, gate, scale, final_head)
    target = velocity_n - (velocity_c - velocity_n)

    def student(branch):
        velocity_s = head_out(branch, image_states, gate, scale, final_head)
        return jnp.sum((velocity_s - target) ** 2) / SAMPLES

    loss_part, pull = jax.vjp(student, branch_s)
    (cotangent,) = pull(jnp.ones_like(loss_part))
    cotangent_samples = cotangent.astype(jnp.bfloat16)
    cotangent_rows = cotangent_samples.reshape(token_rows, WIDTH)
    columns = attention[0]
    return lax.psum_scatter(
        lax.dot_general(
            columns, cotangent_rows, (((0,), (0,)), ((), ())), preferred_element_type=jnp.float32
        ),
        "seq",
        scatter_dimension=0,
        tiled=True,
    )


def solution(mesh):
    return jax.shard_map(
        shards,
        mesh=mesh,
        in_specs=(
            P(None, "grp", None, "seq", None),
            P(None, None, "grp", None, "seq", None),
            P(None, "grp", None),
            P("grp"),
            P("grp", "seq", None),
            P("seq", None),
            P(("grp", "seq"), None),
            P(),
            P(),
        ),
        out_specs=P(("grp", "seq"), None),
        check_vma=False,
    )
```

profile of v0, /device:TPU:0, one launch (start us, length us, event | category | flops | bytes accessed | tf_op | source)
XLA Modules:
  0.0 544.9 jit_solution(13315047425198892459)
XLA Ops:
  7.3 2.2 copy.27
  11.4 7.4 %all-to-all-start.1 = ((bf16[4,64,32,128]{3,2,0,1:T(8,128)(2,1)}), bf16[4,64,32,128]{3,2,0,1:T(8,128)(2,1)}, u32[]{:S(2)}, u32[]{:S(2)}) async-start(bf16[4,64,32,128]{3,2,0,1:T(8,128)(2,1)} %copy.28), calls=%async_computation.1 | async-start | bytes 4194304 | tf_op jit(solution)/shard_map/all_to_all | solution.py:78
  18.9 2.4 copy.23
  23.3 49.5 %all-to-all-done.1 = bf16[4,64,32,128]{3,2,0,1:T(8,128)(2,1)} async-done(((bf16[4,64,32,128]{3,2,0,1:T(8,128)(2,1)}), bf16[4,64,32,128]{3,2,0,1:T(8,128)(2,1)}, u32[]{:S(2)}, u32[]{:S(2)}) %all-to-all-start.1) | async-done | bytes 2097184 | tf_op jit(solution)/shard_map/all_to_all | solution.py:78
  72.8 33.3 %all-to-all-start = ((bf16[3,64,56,128]{3,2,0,1:T(8,128)(2,1)}), bf16[3,64,56,128]{3,2,0,1:T(8,128)(2,1)}, u32[]{:S(2)}, u32[]{:S(2)}) async-start(bf16[3,64,56,128]{3,2,0,1:T(8,128)(2,1)} %copy.24), calls=%async_computation | async-start | bytes 5505024 | tf_op jit(solution)/shard_map/all_to_all | solution.py:77
  107.1 3.4 copy.30
  110.6 72.9 %all-to-all-done = bf16[3,64,56,128]{3,2,0,1:T(8,128)(2,1)} async-done(((bf16[3,64,56,128]{3,2,0,1:T(8,128)(2,1)}), bf16[3,64,56,128]{3,2,0,1:T(8,128)(2,1)}, u32[]{:S(2)}, u32[]{:S(2)}) %all-to-all-start) | async-done | bytes 2752544 | tf_op jit(solution)/shard_map/all_to_all | solution.py:77
  183.5 4.0 copy.26
  187.4 113.6 %while.23 = (s32[]{:T(128)}, bf16[4,2,896,128]{3,1,0,2:T(2,128)(2,1)}, s32[4]{0:T(128)S(1)}, bf16[3,4,896,128]{3,2,1,0:T(8,128)(2,1)}, pred[2,4,512]{2,1,0:T(4,1...) while((s32[]{:T(128)}, ...), condition=%wide.region_9.10_spmd, body=%wide.region_0.9_spmd.sunk | while | flops 447742848 | bytes 26686016 | solution.py:116
  193.9 19.6 %while.24 = (s32[]{:T(128)}, bf16[2,2,448,128]{3,2,1,0:T(8,128)(2,1)}, bf16[2,448,128]{2,1,0:T(8,128)(2,1)S(1)}, bf16[896,128]{1,0:T(8,128)(2,1)}, pred[1,1,512]...) while((s32[]{:T(128)}, ...), condition=%wide.region_8.8_spmd, body=%wide.region_1.7_spmd.sunk | while | flops 447742848 | bytes 22390328 | solution.py:113
  195.9 2.1 fusion.139
  222.3 19.6 %while.24 = (s32[]{:T(128)}, bf16[2,2,448,128]{3,2,1,0:T(8,128)(2,1)}, bf16[2,448,128]{2,1,0:T(8,128)(2,1)S(1)}, bf16[896,128]{1,0:T(8,128)(2,1)}, pred[1,1,512]...) while((s32[]{:T(128)}, ...), condition=%wide.region_8.8_spmd, body=%wide.region_1.7_spmd.sunk | while | flops 447742848 | bytes 22390328 | solution.py:113
  250.7 19.6 %while.24 = (s32[]{:T(128)}, bf16[2,2,448,128]{3,2,1,0:T(8,128)(2,1)}, bf16[2,448,128]{2,1,0:T(8,128)(2,1)S(1)}, bf16[896,128]{1,0:T(8,128)(2,1)}, pred[1,1,512]...) while((s32[]{:T(128)}, ...), condition=%wide.region_8.8_spmd, body=%wide.region_1.7_spmd.sunk | while | flops 447742848 | bytes 22390328 | solution.py:113
  279.1 19.6 %while.24 = (s32[]{:T(128)}, bf16[2,2,448,128]{3,2,1,0:T(8,128)(2,1)}, bf16[2,448,128]{2,1,0:T(8,128)(2,1)S(1)}, bf16[896,128]{1,0:T(8,128)(2,1)}, pred[1,1,512]...) while((s32[]{:T(128)}, ...), condition=%wide.region_8.8_spmd, body=%wide.region_1.7_spmd.sunk | while | flops 447742848 | bytes 22390328 | solution.py:113
  301.1 27.2 %all-to-all-start.2 = ((bf16[2,4,896,128]{3,0,1,2:T(2,128)(2,1)}), bf16[2,4,896,128]{3,0,1,2:T(2,128)(2,1)}, u32[]{:S(2)}, u32[]{:S(2)}) async-start(bf16[2,4,896,128]{3,0,1,2:T(2,128)(2,1)} %bitcast.168), calls=%async_computation.2 | async-start | bytes 3670016 | tf_op jit(solution)/shard_map/all_to_all | solution.py:119
  329.4 35.5 %all-to-all-done.2 = bf16[2,4,896,128]{3,0,1,2:T(2,128)(2,1)} async-done(((bf16[2,4,896,128]{3,0,1,2:T(2,128)(2,1)}), bf16[2,4,896,128]{3,0,1,2:T(2,128)(2,1)}, u32[]{:S(2)}, u32[]{:S(2)}) %all-to-all-start.2) | async-done | bytes 1835040 | tf_op jit(solution)/shard_map/all_to_all | solution.py:119
  364.9 2.7 copy.44
  370.1 2.2 dot_general.69
  372.4 4.9 multiply_reduce_fusion.4
  377.3 5.0 multiply_reduce_fusion.3
  382.7 2.8 multiply_reduce_fusion.2
  386.4 3.4 multiply_reduce_fusion.1
  391.6 6.4 %fusion.70 = f32[2048,1536]{1,0:T(8,128)} fusion(bf16[224,1536]{1,0:T(8,128)(2,1)S(1)} %bitcast.167, bf16[28,8,16,128]{3,2,1,0:T(8,128)(2,1)S(1)} %bitcast.164), kind=kOutput, calls=%fused_computation.90 | convolution fusion | flops 1409286144 | bytes 14188544 | tf_op jit(solution)/shard_map/dot_general | solution.py:153
  398.0 140.3 %reduce-scatter.2.cloned.1.call-done = f32[128,1536]{1,0:T(8,128)} async-done(((f32[2048,1536]{1,0:T(8,128)}), f32[128,1536]{1,0:T(8,128)}) %reduce-scatter.2.cloned.1.call-update) | async-done | bytes 786448 | tf_op jit(solution)/shard_map/reduce_scatter | solution.py:152
  (305 shorter events, 115.1 us)
Async XLA Ops:
  6.5 322.1 %copy-start = (bf16[256,3072]{1,0:T(8,128)(2,1)S(1)}, bf16[256,3072]{1,0:T(8,128)(2,1)}, u32[]{:S(2)}) copy-start(bf16[256,3072]{1,0:T(8,128)(2,1)} %param.20) | copy-start | bytes 4718596
  6.5 365.8 %all-gather.3.cloned.1.call-start = ((), (), s32[]{:S(2)}) async-start(), calls=%async_computation.4 | async-start | bytes 6684672 | tf_op jit(solution)/shard_map/all_gather | solution.py:130
  11.4 61.4 %all-to-all-start.1 = ((bf16[4,64,32,128]{3,2,0,1:T(8,128)(2,1)}), bf16[4,64,32,128]{3,2,0,1:T(8,128)(2,1)}, u32[]{:S(2)}, u32[]{:S(2)}) async-start(bf16[4,64,32,128]{3,2,0,1:T(8,128)(2,1)} %copy.28), calls=%async_computation.1 | async-start | bytes 4194304 | tf_op jit(solution)/shard_map/all_to_all | solution.py:78
  23.3 83.6 %copy-start.15 = (s32[2,4,512]{2,1,0:T(4,128)S(1)}, s32[2,4,512]{2,1,0:T(4,128)}, u32[]{:S(2)}) copy-start(s32[2,4,512]{2,1,0:T(4,128)} %param.15) | copy-start | bytes 49156
  72.8 110.7 %all-to-all-start = ((bf16[3,64,56,128]{3,2,0,1:T(8,128)(2,1)}), bf16[3,64,56,128]{3,2,0,1:T(8,128)(2,1)}, u32[]{:S(2)}, u32[]{:S(2)}) async-start(bf16[3,64,56,128]{3,2,0,1:T(8,128)(2,1)} %copy.24), calls=%async_computation | async-start | bytes 5505024 | tf_op jit(solution)/shard_map/all_to_all | solution.py:77
  106.1 271.1 %all-gather.5.cloned.1.call-start = ((), (), s32[]{:S(2)}) async-start(), calls=%async_computation.5 | async-start | bytes 6684672 | tf_op jit(solution)/shard_map/all_gather | solution.py:129
  187.4 2.5 copy-start.17
  187.4 6.4 %copy-start.11 = (pred[2,4,512]{2,1,0:T(4,128)(4,1)}, pred[2,4,512]{2,1,0:T(4,128)(4,1)S(1)}, u32[]{:S(2)}) copy-start(pred[2,4,512]{2,1,0:T(4,128)(4,1)S(1)} %get-tuple-element.467) | copy-start | bytes 12292 | tf_op jit(solution)/shard_map/while
  215.9 2.5 copy-start.17
  215.9 6.4 %copy-start.11 = (pred[2,4,512]{2,1,0:T(4,128)(4,1)}, pred[2,4,512]{2,1,0:T(4,128)(4,1)S(1)}, u32[]{:S(2)}) copy-start(pred[2,4,512]{2,1,0:T(4,128)(4,1)S(1)} %get-tuple-element.467) | copy-start | bytes 12292 | tf_op jit(solution)/shard_map/while
  241.9 2.4 copy-start.12
  241.9 2.4 copy-start.18
  244.3 2.5 copy-start.17
  244.3 6.4 %copy-start.11 = (pred[2,4,512]{2,1,0:T(4,128)(4,1)}, pred[2,4,512]{2,1,0:T(4,128)(4,1)S(1)}, u32[]{:S(2)}) copy-start(pred[2,4,512]{2,1,0:T(4,128)(4,1)S(1)} %get-tuple-element.467) | copy-start | bytes 12292 | tf_op jit(solution)/shard_map/while
  272.7 2.5 copy-start.17
  272.7 6.4 %copy-start.11 = (pred[2,4,512]{2,1,0:T(4,128)(4,1)}, pred[2,4,512]{2,1,0:T(4,128)(4,1)S(1)}, u32[]{:S(2)}) copy-start(pred[2,4,512]{2,1,0:T(4,128)(4,1)S(1)} %get-tuple-element.467) | copy-start | bytes 12292 | tf_op jit(solution)/shard_map/while
  301.1 27.4 %copy-start.16 = (s32[4]{0:T(128)S(1)}, s32[4]{0:T(128)}, u32[]{:S(2)}) copy-start(s32[4]{0:T(128)} %param.16) | copy-start | bytes 52
  301.1 63.8 %all-to-all-start.2 = ((bf16[2,4,896,128]{3,0,1,2:T(2,128)(2,1)}), bf16[2,4,896,128]{3,0,1,2:T(2,128)(2,1)}, u32[]{:S(2)}, u32[]{:S(2)}) async-start(bf16[2,4,896,128]{3,0,1,2:T(2,128)(2,1)} %bitcast.168), calls=%async_computation.2 | async-start | bytes 3670016 | tf_op jit(solution)/shard_map/all_to_all | solution.py:119
  328.2 210.1 %reduce-scatter.2.cloned.1.call-start = ((), (), s32[]{:S(2)}) async-start(), calls=%async_computation.6 | async-start | bytes 13369344 | tf_op jit(solution)/shard_map/reduce_scatter | solution.py:152
  368.8 3.6 copy-start.5
  377.3 5.1 copy-start.10
  377.3 5.3 copy-start.13
  377.3 5.4 copy-start.14
  382.7 2.9 copy-start.9
  (55 other events, 66.2 us)
Sparse Core Ops, SparseCore 0:
  9.6 98.0 all-gather.2
  110.0 94.7 all-gather.4
  398.2 140.1 reduce-scatter.1
where the time goes:
time: 547 us; the launch traced here: 545 us
  waiting for transfers between devices  300 us (55%)
  matrix products  71 us (13%)
  starting transfers between devices  68.2 us (12%)
  local copies, waits for them, and re-layouts  63.1 us (12%)
  other arithmetic  20.9 us (4%)
  between operations  13.3 us (2%)
  loops' own time  8.68 us (2%)
    reduce_scatter x1, waiting for transfers between devices, shards(): lax.psum_scatter(lax.dot_general(columns, cotangent_rows, (((0,), (0,)),...  140 us
    all_to_all x1, waiting for transfers between devices, shards(): lax.all_to_all(image_local, 'seq', split_axis=1, concat_axis=2, tiled=True)  72.9 us
    all_to_all x1, waiting for transfers between devices, shards(): lax.all_to_all(text_local, 'seq', split_axis=1, concat_axis=2, tiled=True)  49.5 us
    all_to_all x1, waiting for transfers between devices, shards(): lax.all_to_all(both_passes, 'seq', split_axis=2, concat_axis=1, tiled=True)  35.5 us
    all_to_all x1, starting transfers between devices, shards(): lax.all_to_all(image_local, 'seq', split_axis=1, concat_axis=2, tiled=True)  33.3 us
    all_to_all x1, starting transfers between devices, shards(): lax.all_to_all(both_passes, 'seq', split_axis=2, concat_axis=1, tiled=True)  27.2 us
    dot_general x16, matrix products, text_finish(): jnp.dot(queries, text_keys.T, preferred_element_type=jnp.float32) * factor  25.9 us
    while x128, local copies, waits for them, and re-layouts  12.1 us
  transfers between devices with their start and end apart: 6, of which 4 were waited for; matrix products, arithmetic and copies ran while one was open for 22% of the time, Pallas kernels for 0%

commit v1 on v0

--- a/solution.py
+++ b/solution.py
@@ -9,6 +9,20 @@
 HEAD_DIM = 128
 WIDTH = 1536
 TIME_DIM = 256
+
+
+def _hold_notes(unit, row_dim, my_data):
+    finding = unit.shape
+    u1 = unit.reshape(
+        *finding[:row_dim], my_data, finding[row_dim] // my_data, *finding[row_dim + 1 :]
+    )
+    return jnp.moveaxis(u1, row_dim, 0)
+
+
+def panel_group(a0, in_dim):
+    raw_out = list(a0.shape[1:])
+    raw_out[in_dim] *= a0.shape[0]
+    return jnp.moveaxis(a0, 0, in_dim).reshape(raw_out)
 
 
 def image_block(queries, image_keys, image_values):
@@ -116,7 +130,18 @@
     both_passes = lax.map(joint_item, jnp.arange(owned_count, dtype=jnp.int32)).transpose(
         1, 0, 2, 3
     )
-    returned = lax.all_to_all(both_passes, "seq", split_axis=2, concat_axis=1, tiled=True)
+    state_next = lax.psum(1, "seq")
+    wide_out = lax.axis_index("seq")
+    base_arr, top = (state_next, wide_out)
+    all_values = _hold_notes(both_passes, 2, base_arr)
+    seen = [all_values[top]]
+    for k0 in [*range(1, base_arr)]:
+        y_new = all_values[top ^ k0]
+        y2 = lax.ppermute(y_new, "seq", [(p, p ^ k0) for p in range(base_arr)])
+        seen.append(y2)
+    p_next = jnp.stack(seen, axis=0)
+    all_values = p_next[top ^ jnp.arange(base_arr)]
+    returned = panel_group(all_values, 1)
     attention = returned.reshape(2, HEADS, SAMPLES, image_dev, HEAD_DIM).transpose(0, 2, 3, 1, 4)
     attention = attention.reshape(2, token_rows, HEADS * HEAD_DIM)
     half_dim = TIME_DIM // 2

time: 547 us -> 503 us (0.920)
  matrix products: 71 us -> 43.3 us
  waiting for transfers between devices: 300 us -> 279 us
  starting transfers between devices: 68.2 us -> 82.4 us
    ppermute x0 -> x15, starting transfers between devices: none -> 41.6 us  [shards(): y2 = lax.ppermute(y_new, 'seq', [(p, p ^ k0) for p in range(base_arr)])]
    all_to_all x1 -> x0, waiting for transfers between devices: 35.5 us -> none  [shards(): lax.all_to_all(both_passes, 'seq', split_axis=2, concat_axis=1, tiled=True)]
    all_to_all x1 -> x0, starting transfers between devices: 27.2 us -> none  [shards(): lax.all_to_all(both_passes, 'seq', split_axis=2, concat_axis=1, tiled=True)]
    dot_general x16, matrix products: 25.9 us -> 6.04 us  [text_finish(): jnp.dot(queries, text_keys.T, preferred_element_type=jnp.float32) * factor]
    ppermute x0 -> x15, waiting for transfers between devices: none -> 14.9 us  [shards(): y2 = lax.ppermute(y_new, 'seq', [(p, p ^ k0) for p in range(base_arr)])]
    while x128 -> x32, local copies, waits for them, and re-layouts: 12.1 us -> 0.95 us
    unnamed x20 -> x48, local copies, waits for them, and re-layouts: 5 us -> 14.7 us
    another operation x20, other arithmetic: 9.54 us -> 0.38 us
  transfers between devices with their start and end apart: 6 -> 20, of which waited for: 4 -> 8; matrix products, arithmetic and copies ran while one was open for 22% -> 19% of each run, Pallas kernels for 0% -> 0%
where the time goes in v1:
time: 503 us; the launch traced here: 502 us
  waiting for transfers between devices  279 us (55%)
  starting transfers between devices  82.4 us (16%)
  local copies, waits for them, and re-layouts  57.9 us (12%)
  matrix products  43.3 us (9%)
  other arithmetic  17.1 us (3%)
  between operations  13.6 us (3%)
  loops' own time  8.16 us (2%)
    reduce_scatter x1, waiting for transfers between devices, shards(): lax.psum_scatter(lax.dot_general(columns, cotangent_rows, (((0,), (0,)),...  142 us
    all_to_all x1, waiting for transfers between devices, shards(): lax.all_to_all(image_local, 'seq', split_axis=1, concat_axis=2, tiled=True)  71.8 us
    all_to_all x1, waiting for transfers between devices, shards(): lax.all_to_all(text_local, 'seq', split_axis=1, concat_axis=2, tiled=True)  49.5 us
    ppermute x15, starting transfers between devices, shards(): y2 = lax.ppermute(y_new, 'seq', [(p, p ^ k0) for p in range(base_arr)])  41.6 us
    all_to_all x1, starting transfers between devices, shards(): lax.all_to_all(image_local, 'seq', split_axis=1, concat_axis=2, tiled=True)  33.3 us
    ppermute x15, waiting for transfers between devices, shards(): y2 = lax.ppermute(y_new, 'seq', [(p, p ^ k0) for p in range(base_arr)])  14.9 us
    unnamed x48, local copies, waits for them, and re-layouts  14.7 us
  transfers between devices with their start and end apart: 20, of which 8 were waited for; matrix products, arithmetic and copies ran while one was open for 19% of the time, Pallas kernels for 0%

profile of v1, /device:TPU:0, one launch (start us, length us, event | category | flops | bytes accessed | tf_op | source)
XLA Modules:
  0.0 501.9 jit_solution(16793743086689737509)
XLA Ops:
  11.4 7.4 %all-to-all-start.1 = ((bf16[4,64,32,128]{3,2,0,1:T(8,128)(2,1)}), bf16[4,64,32,128]{3,2,0,1:T(8,128)(2,1)}, u32[]{:S(2)}, u32[]{:S(2)}) async-start(bf16[4,64,32,128]{3,2,0,1:T(8,128)(2,1)} %copy.62), calls=%async_computation.1 | async-start | bytes 4194304 | tf_op jit(solution)/shard_map/all_to_all | solution.py:92
  23.3 49.5 %all-to-all-done.1 = bf16[4,64,32,128]{3,2,0,1:T(8,128)(2,1)} async-done(((bf16[4,64,32,128]{3,2,0,1:T(8,128)(2,1)}), bf16[4,64,32,128]{3,2,0,1:T(8,128)(2,1)}, u32[]{:S(2)}, u32[]{:S(2)}) %all-to-all-start.1) | async-done | bytes 2097184 | tf_op jit(solution)/shard_map/all_to_all | solution.py:92
  72.8 33.3 %all-to-all-start = ((bf16[3,64,56,128]{3,2,0,1:T(8,128)(2,1)}), bf16[3,64,56,128]{3,2,0,1:T(8,128)(2,1)}, u32[]{:S(2)}, u32[]{:S(2)}) async-start(bf16[3,64,56,128]{3,2,0,1:T(8,128)(2,1)} %copy.58), calls=%async_computation | async-start | bytes 5505024 | tf_op jit(solution)/shard_map/all_to_all | solution.py:91
  108.2 3.5 copy.64
  111.7 71.8 %all-to-all-done = bf16[3,64,56,128]{3,2,0,1:T(8,128)(2,1)} async-done(((bf16[3,64,56,128]{3,2,0,1:T(8,128)(2,1)}), bf16[3,64,56,128]{3,2,0,1:T(8,128)(2,1)}, u32[]{:S(2)}, u32[]{:S(2)}) %all-to-all-start) | async-done | bytes 2752544 | tf_op jit(solution)/shard_map/all_to_all | solution.py:91
  183.5 4.0 copy.60
  187.4 66.0 %while.23 = (s32[]{:T(128)}, bf16[4,2,896,128]{3,2,1,0:T(8,128)(2,1)}, s32[4]{0:T(128)S(1)}, bf16[3,4,896,128]{3,2,1,0:T(8,128)(2,1)}, pred[2,4,512]{2,1,0:T(4,1...) while((s32[]{:T(128)}, ...), condition=%wide.region_9.10_spmd, body=%wide.region_0.9_spmd.sunk | while | flops 447742848 | bytes 18394864 | solution.py:130
  193.1 9.0 %while.24 = (s32[]{:T(128)}, bf16[2,2,448,128]{3,2,1,0:T(8,128)(2,1)}, bf16[2,448,128]{2,1,0:T(8,128)(2,1)S(1)}, bf16[896,128]{1,0:T(8,128)(2,1)S(1)}, pred[1,1,...) while((s32[]{:T(128)}, ...), condition=%wide.region_8.8_spmd, body=%wide.region_1.7_spmd.sunk | while | flops 447742848 | bytes 14132687 | solution.py:127
  209.6 9.0 %while.24 = (s32[]{:T(128)}, bf16[2,2,448,128]{3,2,1,0:T(8,128)(2,1)}, bf16[2,448,128]{2,1,0:T(8,128)(2,1)S(1)}, bf16[896,128]{1,0:T(8,128)(2,1)S(1)}, pred[1,1,...) while((s32[]{:T(128)}, ...), condition=%wide.region_8.8_spmd, body=%wide.region_1.7_spmd.sunk | while | flops 447742848 | bytes 14132687 | solution.py:127
  226.1 9.0 %while.24 = (s32[]{:T(128)}, bf16[2,2,448,128]{3,2,1,0:T(8,128)(2,1)}, bf16[2,448,128]{2,1,0:T(8,128)(2,1)S(1)}, bf16[896,128]{1,0:T(8,128)(2,1)S(1)}, pred[1,1,...) while((s32[]{:T(128)}, ...), condition=%wide.region_8.8_spmd, body=%wide.region_1.7_spmd.sunk | while | flops 447742848 | bytes 14132687 | solution.py:127
  242.6 9.0 %while.24 = (s32[]{:T(128)}, bf16[2,2,448,128]{3,2,1,0:T(8,128)(2,1)}, bf16[2,448,128]{2,1,0:T(8,128)(2,1)S(1)}, bf16[896,128]{1,0:T(8,128)(2,1)S(1)}, pred[1,1,...) while((s32[]{:T(128)}, ...), condition=%wide.region_8.8_spmd, body=%wide.region_1.7_spmd.sunk | while | flops 447742848 | bytes 14132687 | solution.py:127
  255.3 4.1 collective-permute-start
  260.1 12.0 %collective-permute-start.1 = (bf16[2,4,56,128]{3,2,1,0:T(8,128)(2,1)S(1)}, bf16[2,4,56,128]{3,2,1,0:T(8,128)(2,1)S(1)}, u32[]{:S(2)}, u32[]{:S(2)}) collective-permute-start(bf16[2,4,56,128]{3,2,1,0:T(8,128)(2,1)S(1)} %bitcast.260), channel_id=1, source_target_pairs={{0,2},{1,3},{2,0},{3,1},{4,6},{5,7},{6,4},{7,5},{8,10},{9,11},{10,... | collective-permute-start | bytes 344072 | tf_op jit(solution)/shard_map/ppermute | solution.py:140
  272.2 9.9 %collective-permute-start.3 = (bf16[2,4,56,128]{3,2,1,0:T(8,128)(2,1)S(1)}, bf16[2,4,56,128]{3,2,1,0:T(8,128)(2,1)S(1)}, u32[]{:S(2)}, u32[]{:S(2)}) collective-permute-start(bf16[2,4,56,128]{3,2,1,0:T(8,128)(2,1)S(1)} %bitcast.258), channel_id=1, source_target_pairs={{0,4},{1,5},{2,6},{3,7},{4,0},{5,1},{6,2},{7,3},{8,12},{9,13},{10,... | collective-permute-start | bytes 344072 | tf_op jit(solution)/shard_map/ppermute | solution.py:140
  282.4 3.0 collective-permute-start.5
  286.7 2.8 collective-permute-start.7
  297.9 2.5 collective-permute-start.11
  302.6 8.5 %collective-permute-done.8 = bf16[2,4,56,128]{3,2,1,0:T(8,128)(2,1)S(1)} collective-permute-done((bf16[2,4,56,128]{3,2,1,0:T(8,128)(2,1)S(1)}, bf16[2,4,56,128]{3,2,1,0:T(8,128)(2,1)S(1)}, u32[]{:S(2)}, u32[]{:S(2)}) %collective-permute-start.8) | collective-permute-done | bytes 114720 | tf_op jit(solution)/shard_map/ppermute | solution.py:140
  328.6 4.6 multiply_reduce_fusion.4
  333.3 5.0 %multiply_reduce_fusion.3 = (f32[4,56]{1,0:T(4,128)S(1)}, f32[4,56,1536]{2,1,0:T(8,128)S(1)}) fusion(bf16[4,56,2048]{2,1,0:T(8,128)(2,1)} %dot_general.69, bf16[2048,1536]{1,0:T(8,128)(2,1)} %all-gather.5.cloned.1.call-done, f32[4,1536]{1,0:T(4,128)S(1)} %get-tuple-element.232, bf16[4,56,1536]{2,1,0:T(8,128)(2,1)} %param.17), kind=kOutput, calls=%fused_computation.81 | convolution fusion | flops 1411006208 | bytes 9298816 | tf_op jit(solution)/shard_map/dot_general | solution.py:159
  338.5 2.7 multiply_reduce_fusion.2
  342.1 3.4 multiply_reduce_fusion.1
  347.2 6.4 %fusion.70 = f32[2048,1536]{1,0:T(8,128)} fusion(bf16[224,1536]{1,0:T(8,128)(2,1)S(1)} %bitcast.245, bf16[28,8,16,128]{3,2,1,0:T(8,128)(2,1)S(1)} %bitcast.242), kind=kOutput, calls=%fused_computation.90 | convolution fusion | flops 1409286144 | bytes 14188544 | tf_op jit(solution)/shard_map/dot_general | solution.py:178
  353.6 141.8 %reduce-scatter.2.cloned.1.call-done = f32[128,1536]{1,0:T(8,128)} async-done(((f32[2048,1536]{1,0:T(8,128)}), f32[128,1536]{1,0:T(8,128)}) %reduce-scatter.2.cloned.1.call-update) | async-done | bytes 786448 | tf_op jit(solution)/shard_map/reduce_scatter | solution.py:177
  (271 shorter events, 103.9 us)
Async XLA Ops:
  6.5 101.0 %copy-start = (bf16[256,3072]{1,0:T(8,128)(2,1)S(1)}, bf16[256,3072]{1,0:T(8,128)(2,1)}, u32[]{:S(2)}) copy-start(bf16[256,3072]{1,0:T(8,128)(2,1)} %param.20) | copy-start | bytes 4718596
  6.5 322.1 %all-gather.3.cloned.1.call-start = ((), (), s32[]{:S(2)}) async-start(), calls=%async_computation.3 | async-start | bytes 6684672 | tf_op jit(solution)/shard_map/all_gather | solution.py:155
  11.4 61.4 %all-to-all-start.1 = ((bf16[4,64,32,128]{3,2,0,1:T(8,128)(2,1)}), bf16[4,64,32,128]{3,2,0,1:T(8,128)(2,1)}, u32[]{:S(2)}, u32[]{:S(2)}) async-start(bf16[4,64,32,128]{3,2,0,1:T(8,128)(2,1)} %copy.62), calls=%async_computation.1 | async-start | bytes 4194304 | tf_op jit(solution)/shard_map/all_to_all | solution.py:92
  23.3 83.7 %copy-start.9 = (s32[4]{0:T(128)S(1)}, s32[4]{0:T(128)}, u32[]{:S(2)}) copy-start(s32[4]{0:T(128)} %param.16) | copy-start | bytes 52
  23.3 84.0 %copy-start.8 = (s32[2,4,512]{2,1,0:T(4,128)S(1)}, s32[2,4,512]{2,1,0:T(4,128)}, u32[]{:S(2)}) copy-start(s32[2,4,512]{2,1,0:T(4,128)} %param.15) | copy-start | bytes 49156
  72.8 110.7 %all-to-all-start = ((bf16[3,64,56,128]{3,2,0,1:T(8,128)(2,1)}), bf16[3,64,56,128]{3,2,0,1:T(8,128)(2,1)}, u32[]{:S(2)}, u32[]{:S(2)}) async-start(bf16[3,64,56,128]{3,2,0,1:T(8,128)(2,1)} %copy.58), calls=%async_computation | async-start | bytes 5505024 | tf_op jit(solution)/shard_map/all_to_all | solution.py:91
  106.2 227.2 %all-gather.5.cloned.1.call-start = ((), (), s32[]{:S(2)}) async-start(), calls=%async_computation.4 | async-start | bytes 6684672 | tf_op jit(solution)/shard_map/all_gather | solution.py:154
  106.9 388.5 %reduce-scatter.2.cloned.1.call-start = ((), (), s32[]{:S(2)}) async-start(), calls=%async_computation.5 | async-start | bytes 13369344 | tf_op jit(solution)/shard_map/reduce_scatter | solution.py:177
  255.3 27.1 %collective-permute-start = (bf16[2,4,56,128]{3,2,1,0:T(8,128)(2,1)S(1)}, bf16[2,4,56,128]{3,2,1,0:T(8,128)(2,1)S(1)}, u32[]{:S(2)}, u32[]{:S(2)}) collective-permute-start(bf16[2,4,56,128]{3,2,1,0:T(8,128)(2,1)S(1)} %bitcast.261), channel_id=1, source_target_pairs={{0,1},{1,0},{2,3},{3,2},{4,5},{5,4},{6,7},{7,6},{8,9},{9,8},{10,11... | collective-permute-start | bytes 344072 | tf_op jit(solution)/shard_map/ppermute | solution.py:140
  260.1 25.9 %collective-permute-start.1 = (bf16[2,4,56,128]{3,2,1,0:T(8,128)(2,1)S(1)}, bf16[2,4,56,128]{3,2,1,0:T(8,128)(2,1)S(1)}, u32[]{:S(2)}, u32[]{:S(2)}) collective-permute-start(bf16[2,4,56,128]{3,2,1,0:T(8,128)(2,1)S(1)} %bitcast.260), channel_id=1, source_target_pairs={{0,2},{1,3},{2,0},{3,1},{4,6},{5,7},{6,4},{7,5},{8,10},{9,11},{10,... | collective-permute-start | bytes 344072 | tf_op jit(solution)/shard_map/ppermute | solution.py:140
  272.1 14.6 %collective-permute-start.2 = (bf16[2,4,56,128]{3,2,1,0:T(8,128)(2,1)S(1)}, bf16[2,4,56,128]{3,2,1,0:T(8,128)(2,1)S(1)}, u32[]{:S(2)}, u32[]{:S(2)}) collective-permute-start(bf16[2,4,56,128]{3,2,1,0:T(8,128)(2,1)S(1)} %bitcast.259), channel_id=1, source_target_pairs={{0,3},{1,2},{2,1},{3,0},{4,7},{5,6},{6,5},{7,4},{8,11},{9,10},{10,... | collective-permute-start | bytes 344072 | tf_op jit(solution)/shard_map/ppermute | solution.py:140
  272.2 18.0 %collective-permute-start.3 = (bf16[2,4,56,128]{3,2,1,0:T(8,128)(2,1)S(1)}, bf16[2,4,56,128]{3,2,1,0:T(8,128)(2,1)S(1)}, u32[]{:S(2)}, u32[]{:S(2)}) collective-permute-start(bf16[2,4,56,128]{3,2,1,0:T(8,128)(2,1)S(1)} %bitcast.258), channel_id=1, source_target_pairs={{0,4},{1,5},{2,6},{3,7},{4,0},{5,1},{6,2},{7,3},{8,12},{9,13},{10,... | collective-permute-start | bytes 344072 | tf_op jit(solution)/shard_map/ppermute | solution.py:140
  282.2 9.6 %collective-permute-start.4 = (bf16[2,4,56,128]{3,2,1,0:T(8,128)(2,1)S(1)}, bf16[2,4,56,128]{3,2,1,0:T(8,128)(2,1)S(1)}, u32[]{:S(2)}, u32[]{:S(2)}) collective-permute-start(bf16[2,4,56,128]{3,2,1,0:T(8,128)(2,1)S(1)} %bitcast.257), channel_id=1, source_target_pairs={{0,5},{1,4},{2,7},{3,6},{4,1},{5,0},{6,3},{7,2},{8,13},{9,12},{10,... | collective-permute-start | bytes 344072 | tf_op jit(solution)/shard_map/ppermute | solution.py:140
  282.4 12.8 %collective-permute-start.5 = (bf16[2,4,56,128]{3,2,1,0:T(8,128)(2,1)S(1)}, bf16[2,4,56,128]{3,2,1,0:T(8,128)(2,1)S(1)}, u32[]{:S(2)}, u32[]{:S(2)}) collective-permute-start(bf16[2,4,56,128]{3,2,1,0:T(8,128)(2,1)S(1)} %bitcast.256), channel_id=1, source_target_pairs={{0,6},{1,7},{2,4},{3,5},{4,2},{5,3},{6,0},{7,1},{8,14},{9,15},{10,... | collective-permute-start | bytes 344072 | tf_op jit(solution)/shard_map/ppermute | solution.py:140
  286.1 11.9 %collective-permute-start.6 = (bf16[2,4,56,128]{3,2,1,0:T(8,128)(2,1)S(1)}, bf16[2,4,56,128]{3,2,1,0:T(8,128)(2,1)S(1)}, u32[]{:S(2)}, u32[]{:S(2)}) collective-permute-start(bf16[2,4,56,128]{3,2,1,0:T(8,128)(2,1)S(1)} %bitcast.255), channel_id=1, source_target_pairs={{0,7},{1,6},{2,5},{3,4},{4,3},{5,2},{6,1},{7,0},{8,15},{9,14},{10,... | collective-permute-start | bytes 344072 | tf_op jit(solution)/shard_map/ppermute | solution.py:140
  286.7 14.4 %collective-permute-start.7 = (bf16[2,4,56,128]{3,2,1,0:T(8,128)(2,1)S(1)}, bf16[2,4,56,128]{3,2,1,0:T(8,128)(2,1)S(1)}, u32[]{:S(2)}, u32[]{:S(2)}) collective-permute-start(bf16[2,4,56,128]{3,2,1,0:T(8,128)(2,1)S(1)} %bitcast.254), channel_id=1, source_target_pairs={{0,8},{1,9},{2,10},{3,11},{4,12},{5,13},{6,14},{7,15},{8,0},{9,1},... | collective-permute-start | bytes 344072 | tf_op jit(solution)/shard_map/ppermute | solution.py:140
  290.2 20.9 %collective-permute-start.8 = (bf16[2,4,56,128]{3,2,1,0:T(8,128)(2,1)S(1)}, bf16[2,4,56,128]{3,2,1,0:T(8,128)(2,1)S(1)}, u32[]{:S(2)}, u32[]{:S(2)}) collective-permute-start(bf16[2,4,56,128]{3,2,1,0:T(8,128)(2,1)S(1)} %bitcast.253), channel_id=1, source_target_pairs={{0,9},{1,8},{2,11},{3,10},{4,13},{5,12},{6,15},{7,14},{8,1},{9,0},... | collective-permute-start | bytes 344072 | tf_op jit(solution)/shard_map/ppermute | solution.py:140
  291.7 22.3 %collective-permute-start.9 = (bf16[2,4,56,128]{3,2,1,0:T(8,128)(2,1)S(1)}, bf16[2,4,56,128]{3,2,1,0:T(8,128)(2,1)S(1)}, u32[]{:S(2)}, u32[]{:S(2)}) collective-permute-start(bf16[2,4,56,128]{3,2,1,0:T(8,128)(2,1)S(1)} %bitcast.252), channel_id=1, source_target_pairs={{0,10},{1,11},{2,8},{3,9},{4,14},{5,15},{6,12},{7,13},{8,2},{9,3},... | collective-permute-start | bytes 344072 | tf_op jit(solution)/shard_map/ppermute | solution.py:140
  295.3 21.3 %collective-permute-start.10 = (bf16[2,4,56,128]{3,2,1,0:T(8,128)(2,1)S(1)}, bf16[2,4,56,128]{3,2,1,0:T(8,128)(2,1)S(1)}, u32[]{:S(2)}, u32[]{:S(2)}) collective-permute-start(bf16[2,4,56,128]{3,2,1,0:T(8,128)(2,1)S(1)} %bitcast.251), channel_id=1, source_target_pairs={{0,11},{1,10},{2,9},{3,8},{4,15},{5,14},{6,13},{7,12},{8,3},{9,2},... | collective-permute-start | bytes 344072 | tf_op jit(solution)/shard_map/ppermute | solution.py:140
  297.9 19.3 %collective-permute-start.11 = (bf16[2,4,56,128]{3,2,1,0:T(8,128)(2,1)S(1)}, bf16[2,4,56,128]{3,2,1,0:T(8,128)(2,1)S(1)}, u32[]{:S(2)}, u32[]{:S(2)}) collective-permute-start(bf16[2,4,56,128]{3,2,1,0:T(8,128)(2,1)S(1)} %bitcast.250), channel_id=1, source_target_pairs={{0,12},{1,13},{2,14},{3,15},{4,8},{5,9},{6,10},{7,11},{8,4},{9,5},... | collective-permute-start | bytes 344072 | tf_op jit(solution)/shard_map/ppermute | solution.py:140
  301.1 16.8 %collective-permute-start.12 = (bf16[2,4,56,128]{3,2,1,0:T(8,128)(2,1)S(1)}, bf16[2,4,56,128]{3,2,1,0:T(8,128)(2,1)S(1)}, u32[]{:S(2)}, u32[]{:S(2)}) collective-permute-start(bf16[2,4,56,128]{3,2,1,0:T(8,128)(2,1)S(1)} %bitcast.249), channel_id=1, source_target_pairs={{0,13},{1,12},{2,15},{3,14},{4,9},{5,8},{6,11},{7,10},{8,5},{9,4},... | collective-permute-start | bytes 344072 | tf_op jit(solution)/shard_map/ppermute | solution.py:140
  311.1 8.0 %collective-permute-start.13 = (bf16[2,4,56,128]{3,2,1,0:T(8,128)(2,1)S(1)}, bf16[2,4,56,128]{3,2,1,0:T(8,128)(2,1)S(1)}, u32[]{:S(2)}, u32[]{:S(2)}) collective-permute-start(bf16[2,4,56,128]{3,2,1,0:T(8,128)(2,1)S(1)} %bitcast.248), channel_id=1, source_target_pairs={{0,14},{1,15},{2,12},{3,13},{4,10},{5,11},{6,8},{7,9},{8,6},{9,7},... | collective-permute-start | bytes 344072 | tf_op jit(solution)/shard_map/ppermute | solution.py:140
  314.0 7.9 %collective-permute-start.14 = (bf16[2,4,56,128]{3,2,1,0:T(8,128)(2,1)S(1)}, bf16[2,4,56,128]{3,2,1,0:T(8,128)(2,1)S(1)}, u32[]{:S(2)}, u32[]{:S(2)}) collective-permute-start(bf16[2,4,56,128]{3,2,1,0:T(8,128)(2,1)S(1)} %bitcast.247), channel_id=1, source_target_pairs={{0,15},{1,14},{2,13},{3,12},{4,11},{5,10},{6,9},{7,8},{8,7},{9,6},... | collective-permute-start | bytes 344072 | tf_op jit(solution)/shard_map/ppermute | solution.py:140
  353.6 141.8 %copy-start.1 = (bf16[256,3072]{1,0:T(8,128)(2,1)S(1)}, bf16[256,3072]{1,0:T(8,128)(2,1)}, u32[]{:S(2)}) copy-start(bf16[256,3072]{1,0:T(8,128)(2,1)} %param.20) | copy-start | bytes 4718596
  (20 other events, 31.2 us)
Sparse Core Ops, SparseCore 0:
  9.6 98.0 all-gather.2
  110.0 94.7 all-gather.4
  353.8 141.6 reduce-scatter.1
